TPU v7x, 512 devices: a whole 4x8x8 slice. The times are simulated.
512 devices in a mesh: row: 32 (over z, y_hi), mem: 8 (over x, core), lev: 2 (over y_lo).
Axes of the slice: x: 4, y: 8 (y_hi: 4, y_lo: 2; y = y_hi * 2 + y_lo), z: 8, core: 2. Of those that a mesh axis runs over, the one named last changes fastest.
Arguments:
- control_fields: bfloat16 [16, 6, 1024, 2048], P('mem', 'lev', 'row'), may hold values from -6 to 6
- perturbations: bfloat16 [3, 16, 6, 1024, 2048], P(None, 'mem', 'lev', 'row'), may hold values from -1.5 to 1.5
- column_taper: bfloat16 [2048, 2048], P('row'), may hold values from -1 to 2, as said below
- row_taper: bfloat16 [1024, 1024], P('row'), may hold values from -1 to 2, as said below
- courant_numbers: float32 [3, 6, 1024, 2048], P(None, 'lev', 'row', 'mem'), may hold values from -0.3 to 0.3
- tracer_slope: float32 [2, 6, 1024, 2048], P(None, 'lev', 'row', 'mem'), may hold values from -3 to 3
Outputs:
- increment: float32 [3, 6, 1024, 2048], P(None, 'lev', 'row', 'mem')
Inputs may be any that keep to these rules, and one draw needn't show every extreme that they name: `column_taper`: A square matrix. `row_taper`: A square matrix.
All inputs are finite; a program needn't handle non-finite values.
Results may differ from a plain program's by a relative error of at most 0.0048.
Values may be sent and summed in bfloat16 or wider, within the bound.
No kernel may reach another device: no remote copies, remote signals or barrier semaphores. Data moves between devices by JAX's collectives and lax.ppermute only.
A program may use at most 64 MiB of HBM per device.

v0:
```python
import jax
import jax.numpy as jnp
from jax import lax
from jax.sharding import Mesh
from jax.sharding import PartitionSpec as P

STEPS = 4
ROW = ("row_0", "row_1")


def gather_axes(x, axes, dim):
    if not axes:
        return x
    nearer = lax.all_gather(x, axes[-1], axis=dim, tiled=True)
    return gather_axes(nearer, axes[:-1], dim)


def split_up(x, dim, length):
    before, after = (x.shape[:dim], x.shape[dim + 1 :])
    return jnp.moveaxis(x.reshape(*before, length, -1, *after), dim, 0)


def summed_on_arrival(x, axis, dim):
    parts = split_up(x, dim, lax.axis_size(axis))
    arrived = lax.all_to_all(parts, axis, split_axis=0, concat_axis=0, tiled=True)
    return arrived.astype(jnp.float32).sum(axis=0)


def padded_2(x, sides, width):
    edges = {}
    for axis, dim in sides:
        size, length = (lax.axis_size(axis), x.shape[dim])
        up = [(i, (i + 1) % size) for i in range(size - 1)]
        last = lax.slice_in_dim(x, length - width, length, axis=dim)
        first = lax.slice_in_dim(x, 0, width, axis=dim)
        edges[dim] = (
            lax.ppermute(last, axis, up),
            lax.ppermute(first, axis, [(b, a) for a, b in up]),
        )
    done = []
    for _, dim in sides:
        low, high = edges[dim]
        around = [(width, width) if d in done else (0, 0) for d in range(x.ndim)]
        x = jnp.concatenate([jnp.pad(low, around), x, jnp.pad(high, around)], axis=dim)
        done.append(dim)
    return x


def upwind(middle, behind, forward, velocity):
    return jnp.maximum(velocity, 0.0) * (middle - behind) + jnp.minimum(velocity, 0.0) * (
        forward - middle
    )


def advance(present, courant_numbers, tracer_slope, padded):
    middle = padded[:, 1:-1, 1:-1, 1:-1]
    change = upwind(
        middle, padded[:, :-2, 1:-1, 1:-1], padded[:, 2:, 1:-1, 1:-1], courant_numbers[0]
    )
    change = change + upwind(
        middle, padded[:, 1:-1, :-2, 1:-1], padded[:, 1:-1, 2:, 1:-1], courant_numbers[1]
    )
    change = change + upwind(
        middle, padded[:, 1:-1, 1:-1, :-2], padded[:, 1:-1, 1:-1, 2:], courant_numbers[2]
    )
    shifted = present - change
    source = present[0] * tracer_slope[0] + present[1] * tracer_slope[1]
    return jnp.concatenate([shifted[:2], shifted[2:] - source[None]], axis=0)


def on_device(
    control_fields, perturbations, column_taper, row_taper, courant_numbers, tracer_slope
):
    member_count, level_count, row_count, column_count = control_fields.shape
    field_count = member_count * level_count
    flattened = control_fields.reshape(field_count * row_count, column_count)
    first_pass = jnp.dot(
        flattened,
        lax.all_gather(column_taper, ROW, axis=0, tiled=True),
        preferred_element_type=jnp.float32,
    )
    first_pass = first_pass.astype(jnp.bfloat16).reshape(field_count, row_count, column_count)
    row_whole = gather_axes(row_taper, ROW, 0)
    tapered = jnp.einsum(
        "ij,fjc->fic",
        row_whole,
        lax.all_to_all(first_pass, ROW, split_axis=2, concat_axis=1, tiled=True),
        preferred_element_type=jnp.float32,
    )
    localized = lax.all_to_all(
        tapered.astype(jnp.bfloat16), ROW, split_axis=1, concat_axis=2, tiled=True
    )
    localized = localized.reshape(member_count, level_count, row_count, column_count)
    weighted = jnp.einsum(
        "kmlrc,mlrc->klrc", perturbations, localized, preferred_element_type=jnp.float32
    )
    present = summed_on_arrival(weighted.astype(jnp.bfloat16), "mem", 3)
    for advect_step in range(STEPS):
        padded = padded_2(
            present.astype(jnp.bfloat16), ((ROW, 2), ("mem", 3), ("lev", 1)), 1
        ).astype(present.dtype)
        present = advance(present, courant_numbers, tracer_slope, padded)
    return present


def solution(mesh):
    torus = Mesh(
        mesh.devices.reshape(8, 4, mesh.shape["mem"], mesh.shape["lev"]),
        ("row_0", "row_1", "mem", "lev"),
    )
    placed = (
        P("mem", "lev", ROW, None),
        P(None, "mem", "lev", ROW, None),
        P(ROW, None),
        P(ROW, None),
        P(None, "lev", ROW, "mem"),
        P(None, "lev", ROW, "mem"),
    )
    return jax.shard_map(
        on_device,
        mesh=torus,
        in_specs=placed,
        out_specs=P(None, "lev", ROW, "mem"),
        check_vma=False,
    )
```

profile of v0, /device:TPU:73, one launch (start us, length us, event | category | flops | bytes accessed | tf_op | source)
XLA Modules:
  0.0 396.5 jit_solution(15193475571621653589)
XLA Ops:
  6.5 0.7 all-gather.3.cloned.1.call-update
  7.3 13.9 %all_gather.10 = bf16[128,1024]{1,0:T(8,128)(2,1)} all-gather(bf16[32,1024]{1,0:T(8,128)(2,1)} %param.9), channel_id=1, replica_groups=mesh['row_0'=8,'row_1'=4,'mem'=8,'lev'=2] {'row_1'}, dimensions={0}, use_global_device_ids=true | all-gather | bytes 327680 | tf_op jit(solution)/shard_map/all_gather | solution.py:14
  21.2 129.4 %all-gather.3.cloned.1.call-done = bf16[2048,2048]{1,0:T(8,128)(2,1)} async-done(((bf16[64,2048]{1,0:T(8,128)(2,1)}), bf16[2048,2048]{1,0:T(8,128)(2,1)}) %all-gather.3.cloned.1.call-update) | async-done | bytes 8388624 | tf_op jit(solution)/shard_map/all_gather | solution.py:79
  150.6 5.2 %convolution_convert_fusion = bf16[192,2048]{1,0:T(8,128)(2,1)S(1)} fusion(bf16[192,2048]{1,0:T(8,128)(2,1)S(1)} %bitcast.52, bf16[2048,2048]{1,0:T(8,128)(2,1)} %all-gather.3.cloned.1.call-done), kind=kOutput, calls=%fused_computation.1 | convolution fusion | flops 1611005952 | bytes 9961472 | tf_op jit(solution)/shard_map/dot_general | solution.py:77
  155.8 4.2 %copy.22 = bf16[6,32,2048]{1,0,2:T(8,128)(2,1)} copy(bf16[6,32,2048]{2,1,0:T(8,128)(2,1)S(1)} %bitcast.60) | data formatting | bytes 1572864 | tf_op jit(solution)/shard_map/reshape | solution.py:82
  160.0 5.8 %reshape.20 = bf16[32,2,6144]{2,1,0:T(2,128)(2,1)S(1)} reshape(bf16[2048,6,32]{2,1,0:T(8,128)(2,1)} %bitcast.53) | data formatting | bytes 1572864
  165.8 34.5 %all_to_all.38 = bf16[32,2,6144]{2,1,0:T(2,128)(2,1)S(1)} all-to-all(bf16[32,2,6144]{2,1,0:T(2,128)(2,1)S(1)} %reshape.20), channel_id=1, replica_groups=mesh['row_0'=8,'row_1'=4,'mem'=8,'lev'=2] {'row_0','row_1'}, dimensions={0} | all-to-all | bytes 1572864 | tf_op jit(solution)/shard_map/all_to_all | solution.py:87
  200.3 4.1 %reshape.21 = bf16[2048,6,32]{2,1,0:T(8,128)(2,1)} reshape(bf16[32,2,6144]{2,1,0:T(2,128)(2,1)S(1)} %all_to_all.38) | data formatting | bytes 1572864
  204.5 4.2 %copy.24 = bf16[6,32,32,64]{3,2,1,0:T(8,128)(2,1)S(1)} copy(bf16[6,32,32,64]{2,0,3,1:T(8,128)(2,1)} %bitcast.54) | data formatting | bytes 1572864 | tf_op jit(solution)/shard_map/all_to_all | solution.py:87
  208.7 4.3 %fusion.5 = bf16[6,1024,64]{1,2,0:T(8,128)(2,1)} fusion(bf16[6,1024,64]{2,1,0:T(8,128)(2,1)S(1)} %bitcast.59, bf16[1024,1024]{1,0:T(8,128)(2,1)} %all-gather.5.cloned.1.call-done), kind=kOutput, calls=%fused_computation.8 | convolution fusion | flops 805699584 | bytes 3670016 | tf_op jit(solution)/shard_map/ij,fjc->fic/dot_general | solution.py:84
  213.1 2.6 copy.26
  215.7 2.2 reshape.22
  217.8 26.1 %all_to_all.39 = bf16[32,2,6144]{2,1,0:T(2,128)(2,1)} all-to-all(bf16[32,2,6144]{2,1,0:T(2,128)(2,1)} %reshape.22), channel_id=1, replica_groups=mesh['row_0'=8,'row_1'=4,'mem'=8,'lev'=2] {'row_0','row_1'}, dimensions={0} | all-to-all | bytes 1572864 | tf_op jit(solution)/shard_map/all_to_all | solution.py:90
  243.9 3.3 reshape.23
  247.2 2.2 copy.28
  249.4 2.8 reshape.15
  252.2 0.2 bitcast_convert_fusion
  252.4 1.5 copy-done.2
  253.9 0.5 multiply_reduce_fusion
  254.4 0.3 copy.42
  254.8 0.3 copy.29
  255.1 26.8 %all_to_all.40 = bf16[8,3,3,32,256]{4,3,2,1,0:T(8,128)(2,1)S(1)} all-to-all(bf16[8,3,3,32,256]{4,3,2,1,0:T(8,128)(2,1)S(1)} %copy.29), channel_id=1, replica_groups=mesh['row_0'=8,'row_1'=4,'mem'=8,'lev'=2] {'mem'}, dimensions={0} | all-to-all | bytes 2359296 | tf_op jit(solution)/shard_map/all_to_all | solution.py:25
  281.9 0.2 convert_reduce_fusion
  282.2 2.9 collective-permute-start.1
  285.2 3.5 collective-permute-start.2
  288.7 4.8 %collective-permute-start.3 = (bf16[3,3,1,256]{3,2,1,0:T(2,128)(2,1)S(1)}, bf16[3,3,1,256]{3,2,1,0:T(2,128)(2,1)S(1)}, u32[]{:S(2)}, u32[]{:S(2)}) collective-permute-start(bf16[3,3,1,256]{3,2,1,0:T(2,128)(2,1)S(1)} %get-tuple-element.30), channel_id=1, source_target_pairs={{16,0},{32,16},{48,32},{64,48},{80,64},{96,80},{112,96},{128,112},... | collective-permute-start | bytes 13832 | tf_op jit(solution)/shard_map/ppermute | solution.py:38
  293.5 1.3 collective-permute-start
  294.8 10.6 %collective-permute-start.5 = (bf16[3,1,32,256]{3,2,1,0:T(8,128)(2,1)S(1)}, bf16[3,1,32,256]{3,2,1,0:T(8,128)(2,1)S(1)}, u32[]{:S(2)}, u32[]{:S(2)}) collective-permute-start(bf16[3,1,32,256]{3,2,1,0:T(8,128)(2,1)S(1)} %get-tuple-element.32), channel_id=1, source_target_pairs={{1,0},{3,2},{5,4},{7,6},{9,8},{11,10},{13,12},{15,14},{17,16},{19,... | collective-permute-start | bytes 147464 | tf_op jit(solution)/shard_map/ppermute | solution.py:38
  305.4 2.2 collective-permute-start.4
  307.7 3.4 collective-permute-done.4
  311.1 0.4 fusion.21
  311.5 0.5 fusion.70
  312.0 0.3 copy-done.1
  312.5 1.9 collective-permute-start.8
  314.4 6.4 %collective-permute-start.9 = (bf16[3,3,1,256]{3,2,1,0:T(2,128)(2,1)S(1)}, bf16[3,3,1,256]{3,2,1,0:T(2,128)(2,1)S(1)}, u32[]{:S(2)}, u32[]{:S(2)}) collective-permute-start(bf16[3,3,1,256]{3,2,1,0:T(2,128)(2,1)S(1)} %get-tuple-element.24), channel_id=1, source_target_pairs={{16,0},{32,16},{48,32},{64,48},{80,64},{96,80},{112,96},{128,112},... | collective-permute-start | bytes 13832 | tf_op jit(solution)/shard_map/ppermute | solution.py:38
  320.8 1.3 collective-permute-start.6
  322.1 4.0 %collective-permute-start.11 = (bf16[3,1,32,256]{3,2,1,0:T(8,128)(2,1)S(1)}, bf16[3,1,32,256]{3,2,1,0:T(8,128)(2,1)S(1)}, u32[]{:S(2)}, u32[]{:S(2)}) collective-permute-start(bf16[3,1,32,256]{3,2,1,0:T(8,128)(2,1)S(1)} %get-tuple-element.26), channel_id=1, source_target_pairs={{1,0},{3,2},{5,4},{7,6},{9,8},{11,10},{13,12},{15,14},{17,16},{19,... | collective-permute-start | bytes 147464 | tf_op jit(solution)/shard_map/ppermute | solution.py:38
  326.2 3.0 collective-permute-start.7
  329.2 1.4 collective-permute-done.7
  330.6 1.9 collective-permute-start.10
  332.5 4.4 %collective-permute-done.10 = bf16[3,3,32,1]{3,2,1,0:T(8,128)(2,1)S(1)} collective-permute-done((bf16[3,3,32,1]{3,2,1,0:T(8,128)(2,1)S(1)}, bf16[3,3,32,1]{3,2,1,0:T(8,128)(2,1)S(1)}, u32[]{:S(2)}, u32[]{:S(2)}) %collective-permute-start.10) | collective-permute-done | bytes 608 | tf_op jit(solution)/shard_map/ppermute | solution.py:38
  336.9 0.4 fusion.24
  337.3 0.5 fusion.58
  338.0 1.9 collective-permute-start.14
  339.9 6.4 %collective-permute-start.15 = (bf16[3,3,1,256]{3,2,1,0:T(2,128)(2,1)S(1)}, bf16[3,3,1,256]{3,2,1,0:T(2,128)(2,1)S(1)}, u32[]{:S(2)}, u32[]{:S(2)}) collective-permute-start(bf16[3,3,1,256]{3,2,1,0:T(2,128)(2,1)S(1)} %get-tuple-element.18), channel_id=1, source_target_pairs={{16,0},{32,16},{48,32},{64,48},{80,64},{96,80},{112,96},{128,112},... | collective-permute-start | bytes 13832 | tf_op jit(solution)/shard_map/ppermute | solution.py:38
  346.3 1.3 collective-permute-start.12
  347.6 4.0 %collective-permute-start.17 = (bf16[3,1,32,256]{3,2,1,0:T(8,128)(2,1)S(1)}, bf16[3,1,32,256]{3,2,1,0:T(8,128)(2,1)S(1)}, u32[]{:S(2)}, u32[]{:S(2)}) collective-permute-start(bf16[3,1,32,256]{3,2,1,0:T(8,128)(2,1)S(1)} %get-tuple-element.20), channel_id=1, source_target_pairs={{1,0},{3,2},{5,4},{7,6},{9,8},{11,10},{13,12},{15,14},{17,16},{19,... | collective-permute-start | bytes 147464 | tf_op jit(solution)/shard_map/ppermute | solution.py:38
  351.7 3.0 collective-permute-start.13
  354.7 1.4 collective-permute-done.13
  356.1 1.9 collective-permute-start.16
  358.0 4.4 %collective-permute-done.16 = bf16[3,3,32,1]{3,2,1,0:T(8,128)(2,1)S(1)} collective-permute-done((bf16[3,3,32,1]{3,2,1,0:T(8,128)(2,1)S(1)}, bf16[3,3,32,1]{3,2,1,0:T(8,128)(2,1)S(1)}, u32[]{:S(2)}, u32[]{:S(2)}) %collective-permute-start.16) | collective-permute-done | bytes 608 | tf_op jit(solution)/shard_map/ppermute | solution.py:38
  362.4 0.4 fusion.27
  362.8 0.5 fusion.46
  363.5 1.9 collective-permute-start.20
  365.4 6.4 %collective-permute-start.21 = (bf16[3,3,1,256]{3,2,1,0:T(2,128)(2,1)S(1)}, bf16[3,3,1,256]{3,2,1,0:T(2,128)(2,1)S(1)}, u32[]{:S(2)}, u32[]{:S(2)}) collective-permute-start(bf16[3,3,1,256]{3,2,1,0:T(2,128)(2,1)S(1)} %get-tuple-element.12), channel_id=1, source_target_pairs={{16,0},{32,16},{48,32},{64,48},{80,64},{96,80},{112,96},{128,112},... | collective-permute-start | bytes 13832 | tf_op jit(solution)/shard_map/ppermute | solution.py:38
  371.8 1.3 collective-permute-start.18
  373.1 4.0 %collective-permute-start.23 = (bf16[3,1,32,256]{3,2,1,0:T(8,128)(2,1)S(1)}, bf16[3,1,32,256]{3,2,1,0:T(8,128)(2,1)S(1)}, u32[]{:S(2)}, u32[]{:S(2)}) collective-permute-start(bf16[3,1,32,256]{3,2,1,0:T(8,128)(2,1)S(1)} %get-tuple-element.14), channel_id=1, source_target_pairs={{1,0},{3,2},{5,4},{7,6},{9,8},{11,10},{13,12},{15,14},{17,16},{19,... | collective-permute-start | bytes 147464 | tf_op jit(solution)/shard_map/ppermute | solution.py:38
  377.2 3.0 collective-permute-start.19
  380.2 1.4 collective-permute-done.19
  381.6 1.9 collective-permute-start.22
  383.5 4.4 %collective-permute-done.22 = bf16[3,3,32,1]{3,2,1,0:T(8,128)(2,1)S(1)} collective-permute-done((bf16[3,3,32,1]{3,2,1,0:T(8,128)(2,1)S(1)}, bf16[3,3,32,1]{3,2,1,0:T(8,128)(2,1)S(1)}, u32[]{:S(2)}, u32[]{:S(2)}) %collective-permute-start.22) | collective-permute-done | bytes 608 | tf_op jit(solution)/shard_map/ppermute | solution.py:38
  387.9 0.4 fusion.30
  388.3 0.5 fusion.34
  388.9 0.7 pad_maximum_fusion.3
  (52 shorter events, 1.0 us)
Async XLA Ops:
  6.5 144.1 %copy-start = (bf16[2,3,32,2048]{3,2,1,0:T(8,128)(2,1)S(1)}, bf16[2,3,32,2048]{3,2,1,0:T(8,128)(2,1)}, u32[]{:S(2)}) copy-start(bf16[2,3,32,2048]{3,2,1,0:T(8,128)(2,1)} %param.6) | copy-start | bytes 2359300
  6.5 144.1 %all-gather.3.cloned.1.call-start = ((), (), s32[]{:S(2)}) async-start(), calls=%async_computation.3 | async-start | bytes 8650752 | tf_op jit(solution)/shard_map/all_gather | solution.py:79
  7.3 201.5 %all-gather.5.cloned.1.call-start = ((), (), s32[]{:S(2)}) async-start(), calls=%async_computation.4 | async-start | bytes 2359296 | tf_op jit(solution)/shard_map/all_gather | solution.py:14
  252.2 1.7 copy-start.2
  255.1 52.5 %copy-start.3 = (f32[3,3,32,256]{3,2,1,0:T(8,128)S(1)}, f32[3,3,32,256]{3,2,1,0:T(8,128)}, u32[]{:S(2)}) copy-start(f32[3,3,32,256]{3,2,1,0:T(8,128)} %param.10) | copy-start | bytes 884740
  282.2 23.1 %collective-permute-start.1 = (bf16[3,3,32,1]{3,2,1,0:T(8,128)(2,1)S(1)}, bf16[3,3,32,1]{3,2,1,0:T(8,128)(2,1)S(1)}, u32[]{:S(2)}, u32[]{:S(2)}) collective-permute-start(bf16[3,3,32,1]{3,2,1,0:T(8,128)(2,1)S(1)} %get-tuple-element.33), channel_id=1, source_target_pairs={{0,2},{2,4},{4,6},{6,8},{8,10},{10,12},{12,14},{1,3},{3,5},{5,7},{... | collective-permute-start | bytes 1736 | tf_op jit(solution)/shard_map/ppermute | solution.py:37
  285.2 25.9 %collective-permute-start.2 = (bf16[3,3,1,256]{3,2,1,0:T(2,128)(2,1)S(1)}, bf16[3,3,1,256]{3,2,1,0:T(2,128)(2,1)S(1)}, u32[]{:S(2)}, u32[]{:S(2)}) collective-permute-start(bf16[3,3,1,256]{3,2,1,0:T(2,128)(2,1)S(1)} %get-tuple-element.29), channel_id=1, source_target_pairs={{0,16},{16,32},{32,48},{48,64},{64,80},{80,96},{96,112},{112,128},... | collective-permute-start | bytes 13832 | tf_op jit(solution)/shard_map/ppermute | solution.py:37
  288.7 22.3 %collective-permute-start.3 = (bf16[3,3,1,256]{3,2,1,0:T(2,128)(2,1)S(1)}, bf16[3,3,1,256]{3,2,1,0:T(2,128)(2,1)S(1)}, u32[]{:S(2)}, u32[]{:S(2)}) collective-permute-start(bf16[3,3,1,256]{3,2,1,0:T(2,128)(2,1)S(1)} %get-tuple-element.30), channel_id=1, source_target_pairs={{16,0},{32,16},{48,32},{64,48},{80,64},{96,80},{112,96},{128,112},... | collective-permute-start | bytes 13832 | tf_op jit(solution)/shard_map/ppermute | solution.py:38
  293.5 17.6 %collective-permute-start = (bf16[3,1,32,256]{3,2,1,0:T(8,128)(2,1)S(1)}, bf16[3,1,32,256]{3,2,1,0:T(8,128)(2,1)S(1)}, u32[]{:S(2)}, u32[]{:S(2)}) collective-permute-start(bf16[3,1,32,256]{3,2,1,0:T(8,128)(2,1)S(1)} %get-tuple-element.31), channel_id=1, source_target_pairs={{0,1},{2,3},{4,5},{6,7},{8,9},{10,11},{12,13},{14,15},{16,17},{18,... | collective-permute-start | bytes 147464 | tf_op jit(solution)/shard_map/ppermute | solution.py:37
  294.8 16.3 %collective-permute-start.5 = (bf16[3,1,32,256]{3,2,1,0:T(8,128)(2,1)S(1)}, bf16[3,1,32,256]{3,2,1,0:T(8,128)(2,1)S(1)}, u32[]{:S(2)}, u32[]{:S(2)}) collective-permute-start(bf16[3,1,32,256]{3,2,1,0:T(8,128)(2,1)S(1)} %get-tuple-element.32), channel_id=1, source_target_pairs={{1,0},{3,2},{5,4},{7,6},{9,8},{11,10},{13,12},{15,14},{17,16},{19,... | collective-permute-start | bytes 147464 | tf_op jit(solution)/shard_map/ppermute | solution.py:38
  305.4 5.7 %collective-permute-start.4 = (bf16[3,3,32,1]{3,2,1,0:T(8,128)(2,1)S(1)}, bf16[3,3,32,1]{3,2,1,0:T(8,128)(2,1)S(1)}, u32[]{:S(2)}, u32[]{:S(2)}) collective-permute-start(bf16[3,3,32,1]{3,2,1,0:T(8,128)(2,1)S(1)} %get-tuple-element.34), channel_id=1, source_target_pairs={{2,0},{4,2},{6,4},{8,6},{10,8},{12,10},{14,12},{3,1},{5,3},{7,5},{... | collective-permute-start | bytes 1736 | tf_op jit(solution)/shard_map/ppermute | solution.py:38
  311.5 0.9 copy-start.1
  312.5 24.4 %collective-permute-start.8 = (bf16[3,3,1,256]{3,2,1,0:T(2,128)(2,1)S(1)}, bf16[3,3,1,256]{3,2,1,0:T(2,128)(2,1)S(1)}, u32[]{:S(2)}, u32[]{:S(2)}) collective-permute-start(bf16[3,3,1,256]{3,2,1,0:T(2,128)(2,1)S(1)} %get-tuple-element.23), channel_id=1, source_target_pairs={{0,16},{16,32},{32,48},{48,64},{64,80},{80,96},{96,112},{112,128},... | collective-permute-start | bytes 13832 | tf_op jit(solution)/shard_map/ppermute | solution.py:37
  314.4 22.5 %collective-permute-start.9 = (bf16[3,3,1,256]{3,2,1,0:T(2,128)(2,1)S(1)}, bf16[3,3,1,256]{3,2,1,0:T(2,128)(2,1)S(1)}, u32[]{:S(2)}, u32[]{:S(2)}) collective-permute-start(bf16[3,3,1,256]{3,2,1,0:T(2,128)(2,1)S(1)} %get-tuple-element.24), channel_id=1, source_target_pairs={{16,0},{32,16},{48,32},{64,48},{80,64},{96,80},{112,96},{128,112},... | collective-permute-start | bytes 13832 | tf_op jit(solution)/shard_map/ppermute | solution.py:38
  320.8 16.1 %collective-permute-start.6 = (bf16[3,1,32,256]{3,2,1,0:T(8,128)(2,1)S(1)}, bf16[3,1,32,256]{3,2,1,0:T(8,128)(2,1)S(1)}, u32[]{:S(2)}, u32[]{:S(2)}) collective-permute-start(bf16[3,1,32,256]{3,2,1,0:T(8,128)(2,1)S(1)} %get-tuple-element.25), channel_id=1, source_target_pairs={{0,1},{2,3},{4,5},{6,7},{8,9},{10,11},{12,13},{14,15},{16,17},{18,... | collective-permute-start | bytes 147464 | tf_op jit(solution)/shard_map/ppermute | solution.py:37
  322.1 14.8 %collective-permute-start.11 = (bf16[3,1,32,256]{3,2,1,0:T(8,128)(2,1)S(1)}, bf16[3,1,32,256]{3,2,1,0:T(8,128)(2,1)S(1)}, u32[]{:S(2)}, u32[]{:S(2)}) collective-permute-start(bf16[3,1,32,256]{3,2,1,0:T(8,128)(2,1)S(1)} %get-tuple-element.26), channel_id=1, source_target_pairs={{1,0},{3,2},{5,4},{7,6},{9,8},{11,10},{13,12},{15,14},{17,16},{19,... | collective-permute-start | bytes 147464 | tf_op jit(solution)/shard_map/ppermute | solution.py:38
  326.2 4.4 %collective-permute-start.7 = (bf16[3,3,32,1]{3,2,1,0:T(8,128)(2,1)S(1)}, bf16[3,3,32,1]{3,2,1,0:T(8,128)(2,1)S(1)}, u32[]{:S(2)}, u32[]{:S(2)}) collective-permute-start(bf16[3,3,32,1]{3,2,1,0:T(8,128)(2,1)S(1)} %get-tuple-element.27), channel_id=1, source_target_pairs={{0,2},{2,4},{4,6},{6,8},{8,10},{10,12},{12,14},{1,3},{3,5},{5,7},{... | collective-permute-start | bytes 1736 | tf_op jit(solution)/shard_map/ppermute | solution.py:37
  330.6 6.3 %collective-permute-start.10 = (bf16[3,3,32,1]{3,2,1,0:T(8,128)(2,1)S(1)}, bf16[3,3,32,1]{3,2,1,0:T(8,128)(2,1)S(1)}, u32[]{:S(2)}, u32[]{:S(2)}) collective-permute-start(bf16[3,3,32,1]{3,2,1,0:T(8,128)(2,1)S(1)} %get-tuple-element.28), channel_id=1, source_target_pairs={{2,0},{4,2},{6,4},{8,6},{10,8},{12,10},{14,12},{3,1},{5,3},{7,5},{... | collective-permute-start | bytes 1736 | tf_op jit(solution)/shard_map/ppermute | solution.py:38
  338.0 24.4 %collective-permute-start.14 = (bf16[3,3,1,256]{3,2,1,0:T(2,128)(2,1)S(1)}, bf16[3,3,1,256]{3,2,1,0:T(2,128)(2,1)S(1)}, u32[]{:S(2)}, u32[]{:S(2)}) collective-permute-start(bf16[3,3,1,256]{3,2,1,0:T(2,128)(2,1)S(1)} %get-tuple-element.17), channel_id=1, source_target_pairs={{0,16},{16,32},{32,48},{48,64},{64,80},{80,96},{96,112},{112,128},... | collective-permute-start | bytes 13832 | tf_op jit(solution)/shard_map/ppermute | solution.py:37
  339.9 22.5 %collective-permute-start.15 = (bf16[3,3,1,256]{3,2,1,0:T(2,128)(2,1)S(1)}, bf16[3,3,1,256]{3,2,1,0:T(2,128)(2,1)S(1)}, u32[]{:S(2)}, u32[]{:S(2)}) collective-permute-start(bf16[3,3,1,256]{3,2,1,0:T(2,128)(2,1)S(1)} %get-tuple-element.18), channel_id=1, source_target_pairs={{16,0},{32,16},{48,32},{64,48},{80,64},{96,80},{112,96},{128,112},... | collective-permute-start | bytes 13832 | tf_op jit(solution)/shard_map/ppermute | solution.py:38
  346.3 16.1 %collective-permute-start.12 = (bf16[3,1,32,256]{3,2,1,0:T(8,128)(2,1)S(1)}, bf16[3,1,32,256]{3,2,1,0:T(8,128)(2,1)S(1)}, u32[]{:S(2)}, u32[]{:S(2)}) collective-permute-start(bf16[3,1,32,256]{3,2,1,0:T(8,128)(2,1)S(1)} %get-tuple-element.19), channel_id=1, source_target_pairs={{0,1},{2,3},{4,5},{6,7},{8,9},{10,11},{12,13},{14,15},{16,17},{18,... | collective-permute-start | bytes 147464 | tf_op jit(solution)/shard_map/ppermute | solution.py:37
  347.6 14.8 %collective-permute-start.17 = (bf16[3,1,32,256]{3,2,1,0:T(8,128)(2,1)S(1)}, bf16[3,1,32,256]{3,2,1,0:T(8,128)(2,1)S(1)}, u32[]{:S(2)}, u32[]{:S(2)}) collective-permute-start(bf16[3,1,32,256]{3,2,1,0:T(8,128)(2,1)S(1)} %get-tuple-element.20), channel_id=1, source_target_pairs={{1,0},{3,2},{5,4},{7,6},{9,8},{11,10},{13,12},{15,14},{17,16},{19,... | collective-permute-start | bytes 147464 | tf_op jit(solution)/shard_map/ppermute | solution.py:38
  351.7 4.4 %collective-permute-start.13 = (bf16[3,3,32,1]{3,2,1,0:T(8,128)(2,1)S(1)}, bf16[3,3,32,1]{3,2,1,0:T(8,128)(2,1)S(1)}, u32[]{:S(2)}, u32[]{:S(2)}) collective-permute-start(bf16[3,3,32,1]{3,2,1,0:T(8,128)(2,1)S(1)} %get-tuple-element.21), channel_id=1, source_target_pairs={{0,2},{2,4},{4,6},{6,8},{8,10},{10,12},{12,14},{1,3},{3,5},{5,7},{... | collective-permute-start | bytes 1736 | tf_op jit(solution)/shard_map/ppermute | solution.py:37
  356.1 6.3 %collective-permute-start.16 = (bf16[3,3,32,1]{3,2,1,0:T(8,128)(2,1)S(1)}, bf16[3,3,32,1]{3,2,1,0:T(8,128)(2,1)S(1)}, u32[]{:S(2)}, u32[]{:S(2)}) collective-permute-start(bf16[3,3,32,1]{3,2,1,0:T(8,128)(2,1)S(1)} %get-tuple-element.22), channel_id=1, source_target_pairs={{2,0},{4,2},{6,4},{8,6},{10,8},{12,10},{14,12},{3,1},{5,3},{7,5},{... | collective-permute-start | bytes 1736 | tf_op jit(solution)/shard_map/ppermute | solution.py:38
  363.5 24.4 %collective-permute-start.20 = (bf16[3,3,1,256]{3,2,1,0:T(2,128)(2,1)S(1)}, bf16[3,3,1,256]{3,2,1,0:T(2,128)(2,1)S(1)}, u32[]{:S(2)}, u32[]{:S(2)}) collective-permute-start(bf16[3,3,1,256]{3,2,1,0:T(2,128)(2,1)S(1)} %get-tuple-element.11), channel_id=1, source_target_pairs={{0,16},{16,32},{32,48},{48,64},{64,80},{80,96},{96,112},{112,128},... | collective-permute-start | bytes 13832 | tf_op jit(solution)/shard_map/ppermute | solution.py:37
  365.4 22.4 %collective-permute-start.21 = (bf16[3,3,1,256]{3,2,1,0:T(2,128)(2,1)S(1)}, bf16[3,3,1,256]{3,2,1,0:T(2,128)(2,1)S(1)}, u32[]{:S(2)}, u32[]{:S(2)}) collective-permute-start(bf16[3,3,1,256]{3,2,1,0:T(2,128)(2,1)S(1)} %get-tuple-element.12), channel_id=1, source_target_pairs={{16,0},{32,16},{48,32},{64,48},{80,64},{96,80},{112,96},{128,112},... | collective-permute-start | bytes 13832 | tf_op jit(solution)/shard_map/ppermute | solution.py:38
  371.8 16.1 %collective-permute-start.18 = (bf16[3,1,32,256]{3,2,1,0:T(8,128)(2,1)S(1)}, bf16[3,1,32,256]{3,2,1,0:T(8,128)(2,1)S(1)}, u32[]{:S(2)}, u32[]{:S(2)}) collective-permute-start(bf16[3,1,32,256]{3,2,1,0:T(8,128)(2,1)S(1)} %get-tuple-element.13), channel_id=1, source_target_pairs={{0,1},{2,3},{4,5},{6,7},{8,9},{10,11},{12,13},{14,15},{16,17},{18,... | collective-permute-start | bytes 147464 | tf_op jit(solution)/shard_map/ppermute | solution.py:37
  373.1 14.8 %collective-permute-start.23 = (bf16[3,1,32,256]{3,2,1,0:T(8,128)(2,1)S(1)}, bf16[3,1,32,256]{3,2,1,0:T(8,128)(2,1)S(1)}, u32[]{:S(2)}, u32[]{:S(2)}) collective-permute-start(bf16[3,1,32,256]{3,2,1,0:T(8,128)(2,1)S(1)} %get-tuple-element.14), channel_id=1, source_target_pairs={{1,0},{3,2},{5,4},{7,6},{9,8},{11,10},{13,12},{15,14},{17,16},{19,... | collective-permute-start | bytes 147464 | tf_op jit(solution)/shard_map/ppermute | solution.py:38
  377.2 4.4 %collective-permute-start.19 = (bf16[3,3,32,1]{3,2,1,0:T(8,128)(2,1)S(1)}, bf16[3,3,32,1]{3,2,1,0:T(8,128)(2,1)S(1)}, u32[]{:S(2)}, u32[]{:S(2)}) collective-permute-start(bf16[3,3,32,1]{3,2,1,0:T(8,128)(2,1)S(1)} %get-tuple-element.15), channel_id=1, source_target_pairs={{0,2},{2,4},{4,6},{6,8},{8,10},{10,12},{12,14},{1,3},{3,5},{5,7},{... | collective-permute-start | bytes 1736 | tf_op jit(solution)/shard_map/ppermute | solution.py:37
  381.6 6.3 %collective-permute-start.22 = (bf16[3,3,32,1]{3,2,1,0:T(8,128)(2,1)S(1)}, bf16[3,3,32,1]{3,2,1,0:T(8,128)(2,1)S(1)}, u32[]{:S(2)}, u32[]{:S(2)}) collective-permute-start(bf16[3,3,32,1]{3,2,1,0:T(8,128)(2,1)S(1)} %get-tuple-element.16), channel_id=1, source_target_pairs={{2,0},{4,2},{6,4},{8,6},{10,8},{12,10},{14,12},{3,1},{5,3},{7,5},{... | collective-permute-start | bytes 1736 | tf_op jit(solution)/shard_map/ppermute | solution.py:38
Sparse Core Ops, SparseCore 0:
  10.5 140.0 all-gather.2
  152.7 55.8 all-gather.4
where the time goes:
time: 398 us; the launch traced here: 396 us
  waiting for transfers between devices  151 us (38%)
  blocking collectives  101 us (25%)
  starting transfers between devices  80.7 us (20%)
  local copies, waits for them, and re-layouts  34.4 us (9%)
  between operations  14 us (4%)
  matrix products  9.51 us (2%)
  other arithmetic  5.67 us (1%)
    all_gather x1, waiting for transfers between devices, on_device(): lax.all_gather(column_taper, ROW, axis=0, tiled=True)  129 us
    ppermute x12, starting transfers between devices, padded_2(): lax.ppermute(first, axis, [(b, a) for a, b in up])  54.3 us
    all_to_all x1, blocking collectives, on_device(): lax.all_to_all(first_pass, ROW, split_axis=2, concat_axis=1, tiled=True)  34.5 us
    all_to_all x1, blocking collectives, summed_on_arrival(): lax.all_to_all(parts, axis, split_axis=0, concat_axis=0, tiled=True)  26.8 us
    ppermute x12, starting transfers between devices, padded_2(): lax.ppermute(last, axis, up)  26.4 us
    all_to_all x1, blocking collectives, on_device(): lax.all_to_all(tapered.astype(jnp.bfloat16), ROW, split_axis=1, concat_ax...  26.1 us
    unnamed x13, local copies, waits for them, and re-layouts  17.6 us
    ppermute x12, waiting for transfers between devices, padded_2(): lax.ppermute(first, axis, [(b, a) for a, b in up])  16.5 us
  transfers between devices with their start and end apart: 26, of which 8 were waited for; matrix products, arithmetic and copies ran while one was open for 6% of the time, Pallas kernels for 0%

commit v1 on v0

--- a/solution.py
+++ b/solution.py
@@ -76,7 +76,9 @@
     flattened = control_fields.reshape(field_count * row_count, column_count)
     first_pass = jnp.dot(
         flattened,
-        lax.all_gather(column_taper, ROW, axis=0, tiled=True),
+        jnp.concatenate(
+            lax.all_to_all(jnp.stack([column_taper] * lax.axis_size(ROW)), ROW, 0, 0), axis=0
+        ),
         preferred_element_type=jnp.float32,
     )
     first_pass = first_pass.astype(jnp.bfloat16).reshape(field_count, row_count, column_count)

time: 398 us -> 550 us (1.38)
  blocking collectives: 101 us -> 360 us
  waiting for transfers between devices: 151 us -> 31.3 us
  starting transfers between devices: 80.7 us -> 88.5 us
    all_gather x1, blocking collectives: 13.9 us -> 269 us  [gather_axes(): nearer = lax.all_gather(x, axes[-1], axis=dim, tiled=True)]
    all_gather x1 -> x0, waiting for transfers between devices: 129 us -> none  [on_device(): lax.all_gather(column_taper, ROW, axis=0, tiled=True)]
    all_to_all x0 -> x1, starting transfers between devices: none -> 14.1 us  [on_device(): lax.all_to_all(jnp.stack([column_taper] * lax.axis_size(ROW)), ROW, 0, 0)]
    all_gather x1, waiting for transfers between devices: 0.02 us -> 12.7 us  [gather_axes(): nearer = lax.all_gather(x, axes[-1], axis=dim, tiled=True)]
    ppermute x12, starting transfers between devices: 54.3 us -> 48.3 us  [padded_2(): lax.ppermute(first, axis, [(b, a) for a, b in up])]
    unnamed x13 -> x15, local copies, waits for them, and re-layouts: 17.6 us -> 17.6 us
  transfers between devices with their start and end apart: 26 -> 26, of which waited for: 8 -> 8; matrix products, arithmetic and copies ran while one was open for 6% -> 4% of each run, Pallas kernels for 0% -> 0%
where the time goes in v1:
time: 550 us; the launch traced here: 548 us
  blocking collectives  360 us (65%)
  starting transfers between devices  88.5 us (16%)
  local copies, waits for them, and re-layouts  39.8 us (7%)
  waiting for transfers between devices  31.3 us (6%)
  between operations  14 us (3%)
  matrix products  9.51 us (2%)
  other arithmetic  5.67 us (1%)
    all_gather x1, blocking collectives, gather_axes(): nearer = lax.all_gather(x, axes[-1], axis=dim, tiled=True)  269 us
    ppermute x12, starting transfers between devices, padded_2(): lax.ppermute(first, axis, [(b, a) for a, b in up])  48.3 us
    all_to_all x1, blocking collectives, on_device(): lax.all_to_all(first_pass, ROW, split_axis=2, concat_axis=1, tiled=True)  34.9 us
    all_to_all x1, blocking collectives, summed_on_arrival(): lax.all_to_all(parts, axis, split_axis=0, concat_axis=0, tiled=True)  32.3 us
    ppermute x12, starting transfers between devices, padded_2(): lax.ppermute(last, axis, up)  26.1 us
    all_to_all x1, blocking collectives, on_device(): lax.all_to_all(tapered.astype(jnp.bfloat16), ROW, split_axis=1, concat_ax...  23.8 us
    unnamed x15, local copies, waits for them, and re-layouts  17.6 us
    ppermute x12, waiting for transfers between devices, padded_2(): lax.ppermute(first, axis, [(b, a) for a, b in up])  14.4 us
  transfers between devices with their start and end apart: 26, of which 8 were waited for; matrix products, arithmetic and copies ran while one was open for 4% of the time, Pallas kernels for 0%

profile of v1, /device:TPU:73, one launch (start us, length us, event | category | flops | bytes accessed | tf_op | source)
XLA Modules:
  0.0 548.4 jit_solution(2155020482797028526)
XLA Ops:
  6.5 5.3 stack.2
  11.9 14.1 %all-to-all-start = ((bf16[32,64,2048]{2,1,0:T(8,128)(2,1)}), bf16[32,64,2048]{2,1,0:T(8,128)(2,1)}, u32[]{:S(2)}, u32[]{:S(2)}) async-start(bf16[32,64,2048]{2,1,0:T(8,128)(2,1)} %stack.2), calls=%async_computation | async-start | bytes 16777216 | tf_op jit(solution)/shard_map/all_to_all | solution.py:80
  26.1 268.7 %all_gather.6 = bf16[128,1024]{1,0:T(8,128)(2,1)} all-gather(bf16[32,1024]{1,0:T(8,128)(2,1)S(1)} %copy-done.4), channel_id=1, replica_groups=mesh['row_0'=8,'row_1'=4,'mem'=8,'lev'=2] {'row_1'}, dimensions={0}, use_global_device_ids=true | all-gather | bytes 327680 | tf_op jit(solution)/shard_map/all_gather | solution.py:14
  294.8 5.2 convolution_convert_fusion
  300.0 4.2 copy.22
  304.2 5.8 %reshape.26 = bf16[32,2,6144]{2,1,0:T(2,128)(2,1)S(1)} reshape(bf16[2048,6,32]{2,1,0:T(8,128)(2,1)} %bitcast.54) | data formatting | bytes 1572864
  310.0 34.9 %all_to_all.43 = bf16[32,2,6144]{2,1,0:T(2,128)(2,1)S(1)} all-to-all(bf16[32,2,6144]{2,1,0:T(2,128)(2,1)S(1)} %reshape.26), channel_id=1, replica_groups=mesh['row_0'=8,'row_1'=4,'mem'=8,'lev'=2] {'row_0','row_1'}, dimensions={0} | all-to-all | bytes 1572864 | tf_op jit(solution)/shard_map/all_to_all | solution.py:89
  344.9 4.1 reshape.27
  349.0 4.2 copy.24
  353.3 12.7 %all-gather.2.cloned.1.call-done = bf16[1024,1024]{1,0:T(8,128)(2,1)} async-done(((bf16[128,1024]{1,0:T(8,128)(2,1)}), bf16[1024,1024]{1,0:T(8,128)(2,1)}) %all-gather.2.cloned.1.call-update) | async-done | bytes 2097168 | tf_op jit(solution)/shard_map/all_gather | solution.py:14
  365.9 4.3 fusion.5
  370.3 2.6 copy.26
  372.9 2.2 reshape.28
  375.1 23.8 %all_to_all.44 = bf16[32,2,6144]{2,1,0:T(2,128)(2,1)} all-to-all(bf16[32,2,6144]{2,1,0:T(2,128)(2,1)} %reshape.28), channel_id=1, replica_groups=mesh['row_0'=8,'row_1'=4,'mem'=8,'lev'=2] {'row_0','row_1'}, dimensions={0} | all-to-all | bytes 1572864 | tf_op jit(solution)/shard_map/all_to_all | solution.py:92
  398.8 3.3 reshape.29
  402.1 2.2 copy.28
  404.3 2.8 reshape.21
  407.3 1.5 copy-done.2
  408.8 0.5 multiply_reduce_fusion
  409.3 0.3 copy.42
  409.7 0.3 copy.29
  410.0 32.3 %all_to_all.45 = bf16[8,3,3,32,256]{4,3,2,1,0:T(8,128)(2,1)S(1)} all-to-all(bf16[8,3,3,32,256]{4,3,2,1,0:T(8,128)(2,1)S(1)} %copy.29), channel_id=1, replica_groups=mesh['row_0'=8,'row_1'=4,'mem'=8,'lev'=2] {'mem'}, dimensions={0} | all-to-all | bytes 2359296 | tf_op jit(solution)/shard_map/all_to_all | solution.py:25
  442.3 0.2 convert_reduce_fusion
  442.6 2.9 collective-permute-start.1
  445.6 1.9 collective-permute-start.4
  447.5 1.3 collective-permute-start
  448.8 4.8 collective-permute-start.5
  453.6 1.9 collective-permute-start.2
  455.6 6.4 %collective-permute-start.3 = (bf16[3,3,1,256]{3,2,1,0:T(2,128)(2,1)S(1)}, bf16[3,3,1,256]{3,2,1,0:T(2,128)(2,1)S(1)}, u32[]{:S(2)}, u32[]{:S(2)}) collective-permute-start(bf16[3,3,1,256]{3,2,1,0:T(2,128)(2,1)S(1)} %get-tuple-element.30), channel_id=1, source_target_pairs={{16,0},{32,16},{48,32},{64,48},{80,64},{96,80},{112,96},{128,112},... | collective-permute-start | bytes 13832 | tf_op jit(solution)/shard_map/ppermute | solution.py:38
  462.0 0.7 collective-permute-done.3
  462.7 0.4 fusion.21
  463.1 0.5 fusion.70
  463.7 0.3 copy-done.1
  464.2 1.3 collective-permute-start.11
  465.5 1.3 collective-permute-start.6
  466.8 2.2 collective-permute-start.8
  469.0 6.5 %collective-permute-start.9 = (bf16[3,3,1,256]{3,2,1,0:T(2,128)(2,1)S(1)}, bf16[3,3,1,256]{3,2,1,0:T(2,128)(2,1)S(1)}, u32[]{:S(2)}, u32[]{:S(2)}) collective-permute-start(bf16[3,3,1,256]{3,2,1,0:T(2,128)(2,1)S(1)} %get-tuple-element.24), channel_id=1, source_target_pairs={{16,0},{32,16},{48,32},{64,48},{80,64},{96,80},{112,96},{128,112},... | collective-permute-start | bytes 13832 | tf_op jit(solution)/shard_map/ppermute | solution.py:38
  475.6 2.6 collective-permute-start.10
  478.2 4.9 collective-permute-done.10
  483.1 1.9 collective-permute-start.7
  485.0 1.4 collective-permute-done.7
  486.4 0.4 fusion.24
  486.8 0.5 fusion.58
  487.5 1.3 collective-permute-start.12
  488.8 4.3 collective-permute-start.17
  493.1 1.9 collective-permute-start.14
  495.0 6.4 %collective-permute-start.15 = (bf16[3,3,1,256]{3,2,1,0:T(2,128)(2,1)S(1)}, bf16[3,3,1,256]{3,2,1,0:T(2,128)(2,1)S(1)}, u32[]{:S(2)}, u32[]{:S(2)}) collective-permute-start(bf16[3,3,1,256]{3,2,1,0:T(2,128)(2,1)S(1)} %get-tuple-element.18), channel_id=1, source_target_pairs={{16,0},{32,16},{48,32},{64,48},{80,64},{96,80},{112,96},{128,112},... | collective-permute-start | bytes 13832 | tf_op jit(solution)/shard_map/ppermute | solution.py:38
  501.5 5.1 collective-permute-start.13
  506.6 1.4 collective-permute-done.13
  508.0 1.9 collective-permute-start.16
  509.9 4.4 collective-permute-done.16
  514.3 0.4 fusion.27
  514.7 0.5 fusion.46
  515.4 1.3 collective-permute-start.18
  516.7 4.0 collective-permute-start.23
  520.7 1.9 collective-permute-start.20
  522.6 6.4 %collective-permute-start.21 = (bf16[3,3,1,256]{3,2,1,0:T(2,128)(2,1)S(1)}, bf16[3,3,1,256]{3,2,1,0:T(2,128)(2,1)S(1)}, u32[]{:S(2)}, u32[]{:S(2)}) collective-permute-start(bf16[3,3,1,256]{3,2,1,0:T(2,128)(2,1)S(1)} %get-tuple-element.12), channel_id=1, source_target_pairs={{16,0},{32,16},{48,32},{64,48},{80,64},{96,80},{112,96},{128,112},... | collective-permute-start | bytes 13832 | tf_op jit(solution)/shard_map/ppermute | solution.py:38
  529.1 3.0 collective-permute-start.19
  532.1 1.4 collective-permute-done.19
  533.5 1.9 collective-permute-start.22
  535.4 4.4 collective-permute-done.22
  539.8 0.4 fusion.30
  540.2 0.5 fusion.34
  540.8 0.7 pad_maximum_fusion.3
  (54 shorter events, 1.1 us)
Async XLA Ops:
  6.5 288.3 %copy-start = (bf16[2,3,32,2048]{3,2,1,0:T(8,128)(2,1)S(1)}, bf16[2,3,32,2048]{3,2,1,0:T(8,128)(2,1)}, u32[]{:S(2)}) copy-start(bf16[2,3,32,2048]{3,2,1,0:T(8,128)(2,1)} %param.6) | copy-start | bytes 2359300
  11.9 14.2 %copy-start.4 = (bf16[32,1024]{1,0:T(8,128)(2,1)S(1)}, bf16[32,1024]{1,0:T(8,128)(2,1)}, u32[]{:S(2)}) copy-start(bf16[32,1024]{1,0:T(8,128)(2,1)} %param.9) | copy-start | bytes 196612
  11.9 282.9 %all-to-all-start = ((bf16[32,64,2048]{2,1,0:T(8,128)(2,1)}), bf16[32,64,2048]{2,1,0:T(8,128)(2,1)}, u32[]{:S(2)}, u32[]{:S(2)}) async-start(bf16[32,64,2048]{2,1,0:T(8,128)(2,1)} %stack.2), calls=%async_computation | async-start | bytes 16777216 | tf_op jit(solution)/shard_map/all_to_all | solution.py:80
  26.0 340.0 %all-gather.2.cloned.1.call-start = ((), (), s32[]{:S(2)}) async-start(), calls=%async_computation.4 | async-start | bytes 2359296 | tf_op jit(solution)/shard_map/all_gather | solution.py:14
  407.1 1.7 copy-start.2
  410.0 52.0 %copy-start.3 = (f32[3,3,32,256]{3,2,1,0:T(8,128)S(1)}, f32[3,3,32,256]{3,2,1,0:T(8,128)}, u32[]{:S(2)}) copy-start(f32[3,3,32,256]{3,2,1,0:T(8,128)} %param.10) | copy-start | bytes 884740
  442.6 12.9 %collective-permute-start.1 = (bf16[3,3,32,1]{3,2,1,0:T(8,128)(2,1)S(1)}, bf16[3,3,32,1]{3,2,1,0:T(8,128)(2,1)S(1)}, u32[]{:S(2)}, u32[]{:S(2)}) collective-permute-start(bf16[3,3,32,1]{3,2,1,0:T(8,128)(2,1)S(1)} %get-tuple-element.33), channel_id=1, source_target_pairs={{0,2},{2,4},{4,6},{6,8},{8,10},{10,12},{12,14},{1,3},{3,5},{5,7},{... | collective-permute-start | bytes 1736 | tf_op jit(solution)/shard_map/ppermute | solution.py:37
  445.6 16.4 %collective-permute-start.4 = (bf16[3,3,32,1]{3,2,1,0:T(8,128)(2,1)S(1)}, bf16[3,3,32,1]{3,2,1,0:T(8,128)(2,1)S(1)}, u32[]{:S(2)}, u32[]{:S(2)}) collective-permute-start(bf16[3,3,32,1]{3,2,1,0:T(8,128)(2,1)S(1)} %get-tuple-element.34), channel_id=1, source_target_pairs={{2,0},{4,2},{6,4},{8,6},{10,8},{12,10},{14,12},{3,1},{5,3},{7,5},{... | collective-permute-start | bytes 1736 | tf_op jit(solution)/shard_map/ppermute | solution.py:38
  447.5 15.2 %collective-permute-start = (bf16[3,1,32,256]{3,2,1,0:T(8,128)(2,1)S(1)}, bf16[3,1,32,256]{3,2,1,0:T(8,128)(2,1)S(1)}, u32[]{:S(2)}, u32[]{:S(2)}) collective-permute-start(bf16[3,1,32,256]{3,2,1,0:T(8,128)(2,1)S(1)} %get-tuple-element.31), channel_id=1, source_target_pairs={{0,1},{2,3},{4,5},{6,7},{8,9},{10,11},{12,13},{14,15},{16,17},{18,... | collective-permute-start | bytes 147464 | tf_op jit(solution)/shard_map/ppermute | solution.py:37
  448.8 13.9 %collective-permute-start.5 = (bf16[3,1,32,256]{3,2,1,0:T(8,128)(2,1)S(1)}, bf16[3,1,32,256]{3,2,1,0:T(8,128)(2,1)S(1)}, u32[]{:S(2)}, u32[]{:S(2)}) collective-permute-start(bf16[3,1,32,256]{3,2,1,0:T(8,128)(2,1)S(1)} %get-tuple-element.32), channel_id=1, source_target_pairs={{1,0},{3,2},{5,4},{7,6},{9,8},{11,10},{13,12},{15,14},{17,16},{19,... | collective-permute-start | bytes 147464 | tf_op jit(solution)/shard_map/ppermute | solution.py:38
  453.6 8.4 %collective-permute-start.2 = (bf16[3,3,1,256]{3,2,1,0:T(2,128)(2,1)S(1)}, bf16[3,3,1,256]{3,2,1,0:T(2,128)(2,1)S(1)}, u32[]{:S(2)}, u32[]{:S(2)}) collective-permute-start(bf16[3,3,1,256]{3,2,1,0:T(2,128)(2,1)S(1)} %get-tuple-element.29), channel_id=1, source_target_pairs={{0,16},{16,32},{32,48},{48,64},{64,80},{80,96},{96,112},{112,128},... | collective-permute-start | bytes 13832 | tf_op jit(solution)/shard_map/ppermute | solution.py:37
  455.6 7.2 %collective-permute-start.3 = (bf16[3,3,1,256]{3,2,1,0:T(2,128)(2,1)S(1)}, bf16[3,3,1,256]{3,2,1,0:T(2,128)(2,1)S(1)}, u32[]{:S(2)}, u32[]{:S(2)}) collective-permute-start(bf16[3,3,1,256]{3,2,1,0:T(2,128)(2,1)S(1)} %get-tuple-element.30), channel_id=1, source_target_pairs={{16,0},{32,16},{48,32},{64,48},{80,64},{96,80},{112,96},{128,112},... | collective-permute-start | bytes 13832 | tf_op jit(solution)/shard_map/ppermute | solution.py:38
  463.1 0.9 copy-start.1
  464.2 22.2 %collective-permute-start.11 = (bf16[3,1,32,256]{3,2,1,0:T(8,128)(2,1)S(1)}, bf16[3,1,32,256]{3,2,1,0:T(8,128)(2,1)S(1)}, u32[]{:S(2)}, u32[]{:S(2)}) collective-permute-start(bf16[3,1,32,256]{3,2,1,0:T(8,128)(2,1)S(1)} %get-tuple-element.26), channel_id=1, source_target_pairs={{1,0},{3,2},{5,4},{7,6},{9,8},{11,10},{13,12},{15,14},{17,16},{19,... | collective-permute-start | bytes 147464 | tf_op jit(solution)/shard_map/ppermute | solution.py:38
  465.5 20.9 %collective-permute-start.6 = (bf16[3,1,32,256]{3,2,1,0:T(8,128)(2,1)S(1)}, bf16[3,1,32,256]{3,2,1,0:T(8,128)(2,1)S(1)}, u32[]{:S(2)}, u32[]{:S(2)}) collective-permute-start(bf16[3,1,32,256]{3,2,1,0:T(8,128)(2,1)S(1)} %get-tuple-element.25), channel_id=1, source_target_pairs={{0,1},{2,3},{4,5},{6,7},{8,9},{10,11},{12,13},{14,15},{16,17},{18,... | collective-permute-start | bytes 147464 | tf_op jit(solution)/shard_map/ppermute | solution.py:37
  466.8 19.6 %collective-permute-start.8 = (bf16[3,3,1,256]{3,2,1,0:T(2,128)(2,1)S(1)}, bf16[3,3,1,256]{3,2,1,0:T(2,128)(2,1)S(1)}, u32[]{:S(2)}, u32[]{:S(2)}) collective-permute-start(bf16[3,3,1,256]{3,2,1,0:T(2,128)(2,1)S(1)} %get-tuple-element.23), channel_id=1, source_target_pairs={{0,16},{16,32},{32,48},{48,64},{64,80},{80,96},{96,112},{112,128},... | collective-permute-start | bytes 13832 | tf_op jit(solution)/shard_map/ppermute | solution.py:37
  469.0 17.4 %collective-permute-start.9 = (bf16[3,3,1,256]{3,2,1,0:T(2,128)(2,1)S(1)}, bf16[3,3,1,256]{3,2,1,0:T(2,128)(2,1)S(1)}, u32[]{:S(2)}, u32[]{:S(2)}) collective-permute-start(bf16[3,3,1,256]{3,2,1,0:T(2,128)(2,1)S(1)} %get-tuple-element.24), channel_id=1, source_target_pairs={{16,0},{32,16},{48,32},{64,48},{80,64},{96,80},{112,96},{128,112},... | collective-permute-start | bytes 13832 | tf_op jit(solution)/shard_map/ppermute | solution.py:38
  475.6 7.5 %collective-permute-start.10 = (bf16[3,3,32,1]{3,2,1,0:T(8,128)(2,1)S(1)}, bf16[3,3,32,1]{3,2,1,0:T(8,128)(2,1)S(1)}, u32[]{:S(2)}, u32[]{:S(2)}) collective-permute-start(bf16[3,3,32,1]{3,2,1,0:T(8,128)(2,1)S(1)} %get-tuple-element.28), channel_id=1, source_target_pairs={{2,0},{4,2},{6,4},{8,6},{10,8},{12,10},{14,12},{3,1},{5,3},{7,5},{... | collective-permute-start | bytes 1736 | tf_op jit(solution)/shard_map/ppermute | solution.py:38
  483.1 3.3 collective-permute-start.7
  487.5 26.8 %collective-permute-start.12 = (bf16[3,1,32,256]{3,2,1,0:T(8,128)(2,1)S(1)}, bf16[3,1,32,256]{3,2,1,0:T(8,128)(2,1)S(1)}, u32[]{:S(2)}, u32[]{:S(2)}) collective-permute-start(bf16[3,1,32,256]{3,2,1,0:T(8,128)(2,1)S(1)} %get-tuple-element.19), channel_id=1, source_target_pairs={{0,1},{2,3},{4,5},{6,7},{8,9},{10,11},{12,13},{14,15},{16,17},{18,... | collective-permute-start | bytes 147464 | tf_op jit(solution)/shard_map/ppermute | solution.py:37
  488.8 25.5 %collective-permute-start.17 = (bf16[3,1,32,256]{3,2,1,0:T(8,128)(2,1)S(1)}, bf16[3,1,32,256]{3,2,1,0:T(8,128)(2,1)S(1)}, u32[]{:S(2)}, u32[]{:S(2)}) collective-permute-start(bf16[3,1,32,256]{3,2,1,0:T(8,128)(2,1)S(1)} %get-tuple-element.20), channel_id=1, source_target_pairs={{1,0},{3,2},{5,4},{7,6},{9,8},{11,10},{13,12},{15,14},{17,16},{19,... | collective-permute-start | bytes 147464 | tf_op jit(solution)/shard_map/ppermute | solution.py:38
  493.1 21.2 %collective-permute-start.14 = (bf16[3,3,1,256]{3,2,1,0:T(2,128)(2,1)S(1)}, bf16[3,3,1,256]{3,2,1,0:T(2,128)(2,1)S(1)}, u32[]{:S(2)}, u32[]{:S(2)}) collective-permute-start(bf16[3,3,1,256]{3,2,1,0:T(2,128)(2,1)S(1)} %get-tuple-element.17), channel_id=1, source_target_pairs={{0,16},{16,32},{32,48},{48,64},{64,80},{80,96},{96,112},{112,128},... | collective-permute-start | bytes 13832 | tf_op jit(solution)/shard_map/ppermute | solution.py:37
  495.0 19.3 %collective-permute-start.15 = (bf16[3,3,1,256]{3,2,1,0:T(2,128)(2,1)S(1)}, bf16[3,3,1,256]{3,2,1,0:T(2,128)(2,1)S(1)}, u32[]{:S(2)}, u32[]{:S(2)}) collective-permute-start(bf16[3,3,1,256]{3,2,1,0:T(2,128)(2,1)S(1)} %get-tuple-element.18), channel_id=1, source_target_pairs={{16,0},{32,16},{48,32},{64,48},{80,64},{96,80},{112,96},{128,112},... | collective-permute-start | bytes 13832 | tf_op jit(solution)/shard_map/ppermute | solution.py:38
  501.5 6.5 %collective-permute-start.13 = (bf16[3,3,32,1]{3,2,1,0:T(8,128)(2,1)S(1)}, bf16[3,3,32,1]{3,2,1,0:T(8,128)(2,1)S(1)}, u32[]{:S(2)}, u32[]{:S(2)}) collective-permute-start(bf16[3,3,32,1]{3,2,1,0:T(8,128)(2,1)S(1)} %get-tuple-element.21), channel_id=1, source_target_pairs={{0,2},{2,4},{4,6},{6,8},{8,10},{10,12},{12,14},{1,3},{3,5},{5,7},{... | collective-permute-start | bytes 1736 | tf_op jit(solution)/shard_map/ppermute | solution.py:37
  508.0 6.3 %collective-permute-start.16 = (bf16[3,3,32,1]{3,2,1,0:T(8,128)(2,1)S(1)}, bf16[3,3,32,1]{3,2,1,0:T(8,128)(2,1)S(1)}, u32[]{:S(2)}, u32[]{:S(2)}) collective-permute-start(bf16[3,3,32,1]{3,2,1,0:T(8,128)(2,1)S(1)} %get-tuple-element.22), channel_id=1, source_target_pairs={{2,0},{4,2},{6,4},{8,6},{10,8},{12,10},{14,12},{3,1},{5,3},{7,5},{... | collective-permute-start | bytes 1736 | tf_op jit(solution)/shard_map/ppermute | solution.py:38
  515.4 24.4 %collective-permute-start.18 = (bf16[3,1,32,256]{3,2,1,0:T(8,128)(2,1)S(1)}, bf16[3,1,32,256]{3,2,1,0:T(8,128)(2,1)S(1)}, u32[]{:S(2)}, u32[]{:S(2)}) collective-permute-start(bf16[3,1,32,256]{3,2,1,0:T(8,128)(2,1)S(1)} %get-tuple-element.13), channel_id=1, source_target_pairs={{0,1},{2,3},{4,5},{6,7},{8,9},{10,11},{12,13},{14,15},{16,17},{18,... | collective-permute-start | bytes 147464 | tf_op jit(solution)/shard_map/ppermute | solution.py:37
  516.7 23.1 %collective-permute-start.23 = (bf16[3,1,32,256]{3,2,1,0:T(8,128)(2,1)S(1)}, bf16[3,1,32,256]{3,2,1,0:T(8,128)(2,1)S(1)}, u32[]{:S(2)}, u32[]{:S(2)}) collective-permute-start(bf16[3,1,32,256]{3,2,1,0:T(8,128)(2,1)S(1)} %get-tuple-element.14), channel_id=1, source_target_pairs={{1,0},{3,2},{5,4},{7,6},{9,8},{11,10},{13,12},{15,14},{17,16},{19,... | collective-permute-start | bytes 147464 | tf_op jit(solution)/shard_map/ppermute | solution.py:38
  520.7 19.1 %collective-permute-start.20 = (bf16[3,3,1,256]{3,2,1,0:T(2,128)(2,1)S(1)}, bf16[3,3,1,256]{3,2,1,0:T(2,128)(2,1)S(1)}, u32[]{:S(2)}, u32[]{:S(2)}) collective-permute-start(bf16[3,3,1,256]{3,2,1,0:T(2,128)(2,1)S(1)} %get-tuple-element.11), channel_id=1, source_target_pairs={{0,16},{16,32},{32,48},{48,64},{64,80},{80,96},{96,112},{112,128},... | collective-permute-start | bytes 13832 | tf_op jit(solution)/shard_map/ppermute | solution.py:37
  522.6 17.2 %collective-permute-start.21 = (bf16[3,3,1,256]{3,2,1,0:T(2,128)(2,1)S(1)}, bf16[3,3,1,256]{3,2,1,0:T(2,128)(2,1)S(1)}, u32[]{:S(2)}, u32[]{:S(2)}) collective-permute-start(bf16[3,3,1,256]{3,2,1,0:T(2,128)(2,1)S(1)} %get-tuple-element.12), channel_id=1, source_target_pairs={{16,0},{32,16},{48,32},{64,48},{80,64},{96,80},{112,96},{128,112},... | collective-permute-start | bytes 13832 | tf_op jit(solution)/shard_map/ppermute | solution.py:38
  529.1 4.4 collective-permute-start.19
  533.5 6.3 %collective-permute-start.22 = (bf16[3,3,32,1]{3,2,1,0:T(8,128)(2,1)S(1)}, bf16[3,3,32,1]{3,2,1,0:T(8,128)(2,1)S(1)}, u32[]{:S(2)}, u32[]{:S(2)}) collective-permute-start(bf16[3,3,32,1]{3,2,1,0:T(8,128)(2,1)S(1)} %get-tuple-element.16), channel_id=1, source_target_pairs={{2,0},{4,2},{6,4},{8,6},{10,8},{12,10},{14,12},{3,1},{5,3},{7,5},{... | collective-permute-start | bytes 1736 | tf_op jit(solution)/shard_map/ppermute | solution.py:38
Sparse Core Ops, SparseCore 0:
  294.9 70.9 all-gather.1
